TPU v7x, 32 devices: a whole 2x2x4 slice. The times are simulated.
32 devices in a mesh: batch: 4 (over y, core), proto: 8 (over z, x).
Axes of the slice: x: 2, y: 2, z: 4, core: 2. Of those that a mesh axis runs over, the one named last changes fastest.
Arguments:
- features: bfloat16 [4096, 256], P(('batch', 'proto')), may hold values from -8 to 8
- head_weight: bfloat16 [256, 65536], P('batch', 'proto'), may hold values from -0.375 to 0.375
- student_scores: bfloat16 [2, 4096, 65536], P(None, 'batch', 'proto'), may hold values from -1 to 1
Outputs:
- targets: bfloat16 [4096, 65536], P('batch', 'proto')
- row_loss: float32 [2, 4096], P(None, 'batch')
All inputs are finite; a program needn't handle non-finite values.
Results may differ from a plain program's by a relative error of at most 0.0013.
Values may be sent and summed in bfloat16 or wider, within the bound.
No kernel may reach another device: no remote copies, remote signals or barrier semaphores. Data moves between devices by JAX's collectives and lax.ppermute only.
A program may use at most 192 MiB of HBM per device.

v0:
```python
import jax
import jax.numpy as jnp
from jax import lax
from jax.sharding import PartitionSpec as P

PROTOS = 65536
ITERS = 3
TEACHER_TEMP = 0.07
STUDENT_TEMP = 0.1


def normalize_columns(balance):
    column_sum = lax.psum(jnp.sum(balance, axis=0), "batch")
    return balance / column_sum[None, :]


def crop_totals(balance):
    return lax.psum(jnp.sum(balance, axis=1), "proto")


def local(features, head_weight, student_scores):
    gathered = lax.all_gather(features, "proto", axis=0, tiled=True)
    feat_wide = gathered.astype(jnp.float32)
    fnorm = jnp.sqrt(jnp.sum(feat_wide * feat_wide, axis=1) + 1e-06)
    piece = lax.all_gather(head_weight, "batch", axis=0, tiled=True)
    piece_wide = piece.astype(jnp.float32)
    raw = jnp.dot(gathered, piece, preferred_element_type=jnp.float32)
    squares = jnp.sum(piece_wide * piece_wide, axis=0)
    wnorm = jnp.sqrt(squares + 1e-06)
    balance = jnp.exp(raw / (fnorm[:, None] * wnorm[None, :]) / TEACHER_TEMP)
    logits = student_scores.astype(jnp.float32) / STUDENT_TEMP
    exp_sums = jnp.sum(jnp.exp(logits), axis=2)
    for step in range(ITERS - 1):
        balance = normalize_columns(balance)
        balance = balance / crop_totals(balance)[:, None]
    balance = normalize_columns(balance)
    weighted = jnp.sum(logits * balance[None, :, :], axis=2)
    last_rows, total_exp, total_weighted = lax.psum(
        (jnp.sum(balance, axis=1), exp_sums, weighted), "proto"
    )
    balance = balance / last_rows[:, None]
    row_loss = jnp.log(total_exp) - total_weighted / last_rows[None, :]
    targets = (balance * PROTOS).astype(jnp.bfloat16)
    return (targets, row_loss)


def solution(mesh):
    return jax.shard_map(
        local,
        mesh=mesh,
        in_specs=(P(("batch", "proto"), None), P("batch", "proto"), P(None, "batch", "proto")),
        out_specs=(P("batch", "proto"), P(None, "batch")),
        check_vma=False,
    )
```

profile of v0, /device:TPU:0, one launch (start us, length us, event | category | flops | bytes accessed | tf_op | source)
XLA Modules:
  0.0 311.4 jit_solution(16653263350034114309)
XLA Ops:
  7.2 0.0 all-gather.2.cloned.1.call-start
  7.2 0.7 all-gather.2.cloned.1.call-update
  7.9 33.2 %all_gather.6 = bf16[1024,256]{1,0:T(8,128)(2,1)S(1)} all-gather(bf16[128,256]{1,0:T(8,128)(2,1)} %param.3), channel_id=1, replica_groups=mesh['batch'=4,'proto'=8] {'proto'}, dimensions={0}, use_global_device_ids=true | all-gather | bytes 589824 | tf_op jit(solution)/shard_map/all_gather | solution.py:22
  41.1 0.2 multiply_reduce_fusion.1
  41.4 5.4 %all-gather.2.cloned.1.call-done = bf16[256,8192]{1,0:T(8,128)(2,1)} async-done(((bf16[64,8192]{1,0:T(8,128)(2,1)}), bf16[256,8192]{1,0:T(8,128)(2,1)}) %all-gather.2.cloned.1.call-update) | async-done | bytes 4194320 | tf_op jit(solution)/shard_map/all_gather | solution.py:25
  46.7 3.1 multiply_reduce_fusion
  49.8 17.7 %fusion.16 = (f32[8192]{0:T(1024)S(1)}, f32[1024,8192]{1,0:T(8,128)}) fusion(f32[8192]{0:T(1024)S(1)} %add_sqrt_fusion, f32[1024]{0:T(1024)S(1)} %add_sqrt_fusion.1, bf16[1024,256]{1,0:T(8,128)(2,1)S(1)} %all_gather.6, bf16[256,8192]{1,0:T(8,128)(2,1)} %all-gather.2.cloned.1.call-done), kind=kOutput, calls=%fused_computation.28 | convolution fusion | flops 4328513536 | bytes 38342656 | tf_op jit(solution)/shard_map/dot_general | solution.py:27
  67.5 10.4 %psum.56 = f32[8192]{0:T(1024)S(1)} all-reduce(f32[8192]{0:T(1024)S(1)} %get-tuple-element.9), channel_id=1, replica_groups=mesh['batch'=4,'proto'=8] {'batch'}, use_global_device_ids=true, to_apply=%region_3.0 | all-reduce | flops 8192 | bytes 65536 | tf_op jit(solution)/shard_map/psum | solution.py:13
  77.9 12.2 %divide_reduce_fusion = f32[1024]{0:T(1024)S(1)} fusion(f32[1024,8192]{1,0:T(8,128)} %get-tuple-element.10, f32[8192]{0:T(1024)S(1)} %psum.56), kind=kLoop, calls=%fused_computation.16 | loop fusion | flops 16776192 | bytes 33591296 | tf_op jit(solution)/shard_map/reduce_sum | solution.py:18
  90.1 21.5 %psum.57 = f32[1024]{0:T(1024)S(1)} all-reduce(f32[1024]{0:T(1024)S(1)} %divide_reduce_fusion), channel_id=1, replica_groups=mesh['batch'=4,'proto'=8] {'proto'}, use_global_device_ids=true, to_apply=%region_5.0 | all-reduce | flops 1024 | bytes 8192 | tf_op jit(solution)/shard_map/psum | solution.py:18
  111.6 14.1 %fusion.11 = f32[8192]{0:T(1024)S(1)} fusion(f32[1024,8192]{1,0:T(8,128)} %get-tuple-element.10, f32[1024]{0:T(1024)S(1)} %psum.57, f32[8192]{0:T(1024)S(1)} %psum.56), kind=kLoop, calls=%fused_computation.17 | loop fusion | flops 25157632 | bytes 33624064 | tf_op jit(solution)/shard_map/reduce_sum | solution.py:13
  125.7 10.3 %psum.58 = f32[8192]{0:T(1024)S(1)} all-reduce(f32[8192]{0:T(1024)S(1)} %fusion.11), channel_id=1, replica_groups=mesh['batch'=4,'proto'=8] {'batch'}, use_global_device_ids=true, to_apply=%region_7.0 | all-reduce | flops 8192 | bytes 65536 | tf_op jit(solution)/shard_map/psum | solution.py:13
  136.0 14.1 %fusion.13 = f32[1024]{0:T(1024)S(1)} fusion(f32[1024,8192]{1,0:T(8,128)} %get-tuple-element.10, f32[8192]{0:T(1024)S(1)} %psum.58, f32[1024]{0:T(1024)S(1)} %psum.57, f32[8192]{0:T(1024)S(1)} %psum.56), kind=kLoop, calls=%fused_computation.19 | loop fusion | flops 33553408 | bytes 33628160 | tf_op jit(solution)/shard_map/reduce_sum | solution.py:18
  150.1 17.1 %psum.59 = f32[1024]{0:T(1024)S(1)} all-reduce(f32[1024]{0:T(1024)S(1)} %fusion.13), channel_id=1, replica_groups=mesh['batch'=4,'proto'=8] {'proto'}, use_global_device_ids=true, to_apply=%region_9.0 | all-reduce | flops 1024 | bytes 8192 | tf_op jit(solution)/shard_map/psum | solution.py:18
  167.3 14.5 %fusion.14 = f32[8192]{0:T(1024)S(1)} fusion(f32[1024,8192]{1,0:T(8,128)} %get-tuple-element.10, f32[1024]{0:T(1024)S(1)} %psum.59, f32[8192]{0:T(1024)S(1)} %psum.58, f32[1024]{0:T(1024)S(1)} %psum.57, f32[8192]{0:T(1024)S(1)} %psum.56), kind=kLoop, calls=%fused_computation.20 | loop fusion | flops 41934848 | bytes 33660928 | tf_op jit(solution)/shard_map/reduce_sum | solution.py:13
  181.7 10.4 %psum.60 = f32[8192]{0:T(1024)S(1)} all-reduce(f32[8192]{0:T(1024)S(1)} %fusion.14), channel_id=1, replica_groups=mesh['batch'=4,'proto'=8] {'batch'}, use_global_device_ids=true, to_apply=%region_11.0 | all-reduce | flops 8192 | bytes 65536 | tf_op jit(solution)/shard_map/psum | solution.py:13
  192.2 28.0 %broadcast_multiply_fusion = (f32[1024,8192]{1,0:T(8,128)}, f32[1024]{0:T(1024)S(1)}) fusion(f32[1024,8192]{1,0:T(8,128)} %get-tuple-element.10, f32[8192]{0:T(1024)S(1)} %psum.60, f32[1024]{0:T(1024)S(1)} %psum.59, f32[8192]{0:T(1024)S(1)} %psum.58, f32[1024]{0:T(1024)S(1)} %psum.57, f32[8192]{0:T(1024)S(1)} %psum.56), kind=kLoop, calls=%fused_computation.21 | loop fusion | flops 58719232 | bytes 67219456 | tf_op jit(solution)/shard_map/mul | solution.py:37
  220.2 27.8 %fusion.1 = (f32[2,1024]{1,0:T(2,128)S(1)}, f32[2,1024]{1,0:T(2,128)S(1)}) fusion(bf16[2,1024,8192]{2,1,0:T(8,128)(2,1)} %param.5, f32[1024,8192]{1,0:T(8,128)} %get-tuple-element.7), kind=kLoop, calls=%fused_computation.3 | loop fusion | flops 83881984 | bytes 67125248 | tf_op jit(solution)/shard_map/reduce_sum | solution.py:32
  248.0 34.9 %all-reduce = (f32[1024]{0:T(1024)S(1)}, f32[2,1024]{1,0:T(2,128)S(1)}, f32[2,1024]{1,0:T(2,128)S(1)}) all-reduce(f32[1024]{0:T(1024)S(1)} %get-tuple-element.8, f32[2,1024]{1,0:T(2,128)S(1)} %get-tuple-element.3, f32[2,1024]{1,0:T(2,128)S(1)} %get-tuple-element.2), channel_id=1, replica_groups=mesh['batch'=4,'proto'=8] {'proto'}, use_global_device_ids=true, to_apply=%region_13.0 | all-reduce | flops 5120 | bytes 40960 | tf_op jit(solution)/shard_map/psum | solution.py:38
  282.9 21.1 %fusion.12 = bf16[1024,8192]{1,0:T(8,128)(2,1)} fusion(f32[1024,8192]{1,0:T(8,128)} %get-tuple-element.10, f32[1024]{0:T(1024)S(1)} %get-tuple-element.4, f32[8192]{0:T(1024)S(1)} %psum.60, f32[1024]{0:T(1024)S(1)} %psum.59, f32[8192]{0:T(1024)S(1)} %psum.58, f32[1024]{0:T(1024)S(1)} %psum.57, f32[8192]{0:T(1024)S(1)} %psum.56), kind=kLoop, calls=%fused_computation.18 | loop fusion | flops 67108864 | bytes 50442240 | tf_op jit(solution)/shard_map/convert_element_type | solution.py:43
  303.9 0.6 divide_subtract_fusion
  (2 shorter events, 0.0 us)
Async XLA Ops:
  7.2 39.6 %all-gather.2.cloned.1.call-start = ((), (), s32[]{:S(2)}) async-start(), calls=%async_computation | async-start | bytes 5242880 | tf_op jit(solution)/shard_map/all_gather | solution.py:25
Sparse Core Ops, SparseCore 0:
  9.5 37.1 all-gather.1
where the time goes:
time: 312 us; the launch traced here: 311 us
  blocking collectives  138 us (44%)
  other arithmetic  136 us (44%)
  matrix products  17.7 us (6%)
  between operations  14.1 us (5%)
  waiting for transfers between devices  6.05 us (2%)
    psum x2, blocking collectives, crop_totals(): return lax.psum(jnp.sum(balance, axis=1), 'proto')  38.7 us
    psum x1, blocking collectives, local(): lax.psum((jnp.sum(balance, axis=1), exp_sums, weighted), 'proto')  34.9 us
    all_gather x1, blocking collectives, local(): gathered = lax.all_gather(features, 'proto', axis=0, tiled=True)  33.2 us
    psum x3, blocking collectives, normalize_columns(): column_sum = lax.psum(jnp.sum(balance, axis=0), 'batch')  31.1 us
    reduce_sum x2, other arithmetic, normalize_columns(): column_sum = lax.psum(jnp.sum(balance, axis=0), 'batch')  28.5 us
    mul x1, other arithmetic, local(): weighted = jnp.sum(logits * balance[None, :, :], axis=2)  28 us
    reduce_sum x1, other arithmetic, local(): exp_sums = jnp.sum(jnp.exp(logits), axis=2)  27.8 us
    reduce_sum x2, other arithmetic, crop_totals(): return lax.psum(jnp.sum(balance, axis=1), 'proto')  26.3 us
  transfers between devices with their start and end apart: 1, of which 1 were waited for; matrix products, arithmetic and copies ran while one was open for 0% of the time, Pallas kernels for 0%

commit v1 on v0

--- a/solution.py
+++ b/solution.py
@@ -7,6 +7,23 @@
 ITERS = 3
 TEACHER_TEMP = 0.07
 STUDENT_TEMP = 0.1
+
+
+def in_order(tiles, dim):
+    tiles = jnp.moveaxis(tiles, 0, dim)
+    shape = tiles.shape
+    return tiles.reshape(*shape[:dim], shape[dim] * shape[dim + 1], *shape[dim + 2 :])
+
+
+def grow_blocks(x, axis):
+    length, index = (lax.axis_size(axis), lax.axis_index(axis))
+    blocks, bit = (x[None], 1)
+    while bit < length:
+        other = lax.ppermute(blocks, axis, [(i, i ^ bit) for i in range(length)])
+        low = index & bit == 0
+        blocks = jnp.concatenate([jnp.where(low, blocks, other), jnp.where(low, other, blocks)])
+        bit *= 2
+    return blocks
 
 
 def normalize_columns(balance):
@@ -19,7 +36,7 @@
 
 
 def local(features, head_weight, student_scores):
-    gathered = lax.all_gather(features, "proto", axis=0, tiled=True)
+    gathered = in_order(grow_blocks(features, "proto"), 0)
     feat_wide = gathered.astype(jnp.float32)
     fnorm = jnp.sqrt(jnp.sum(feat_wide * feat_wide, axis=1) + 1e-06)
     piece = lax.all_gather(head_weight, "batch", axis=0, tiled=True)

time: 312 us -> 312 us (level)
  blocking collectives: 138 us -> 105 us
  waiting for transfers between devices: 6.05 us -> 30 us
  starting transfers between devices: 0.04 us -> 8.34 us
    all_gather x1 -> x0, blocking collectives: 33.2 us -> none  [local(): gathered = lax.all_gather(features, 'proto', axis=0, tiled=True)]
    ppermute x0 -> x3, waiting for transfers between devices: none -> 15 us  [grow_blocks(): other = lax.ppermute(blocks, axis, [(i, i ^ bit) for i in range(length)])]
    all_gather x1, waiting for transfers between devices: 5.37 us -> 14.2 us  [local(): piece = lax.all_gather(head_weight, 'batch', axis=0, tiled=True)]
    ppermute x0 -> x3, starting transfers between devices: none -> 8.3 us  [grow_blocks(): other = lax.ppermute(blocks, axis, [(i, i ^ bit) for i in range(length)])]
  transfers between devices with their start and end apart: 1 -> 4, of which waited for: 1 -> 4; matrix products, arithmetic and copies ran while one was open for 0% -> 0% of each run, Pallas kernels for 0% -> 0%
where the time goes in v1:
time: 312 us; the launch traced here: 311 us
  other arithmetic  137 us (44%)
  blocking collectives  105 us (34%)
  waiting for transfers between devices  30 us (10%)
  matrix products  17.7 us (6%)
  between operations  14.1 us (5%)
  starting transfers between devices  8.34 us (3%)
    psum x2, blocking collectives, crop_totals(): return lax.psum(jnp.sum(balance, axis=1), 'proto')  38.7 us
    psum x1, blocking collectives, local(): lax.psum((jnp.sum(balance, axis=1), exp_sums, weighted), 'proto')  34.9 us
    psum x3, blocking collectives, normalize_columns(): column_sum = lax.psum(jnp.sum(balance, axis=0), 'batch')  31.1 us
    reduce_sum x2, other arithmetic, normalize_columns(): column_sum = lax.psum(jnp.sum(balance, axis=0), 'batch')  28.5 us
    mul x1, other arithmetic, local(): weighted = jnp.sum(logits * balance[None, :, :], axis=2)  28 us
    reduce_sum x1, other arithmetic, local(): exp_sums = jnp.sum(jnp.exp(logits), axis=2)  27.8 us
    reduce_sum x2, other arithmetic, crop_totals(): return lax.psum(jnp.sum(balance, axis=1), 'proto')  26.3 us
    convert_element_type x1, other arithmetic, local(): targets = (balance * PROTOS).astype(jnp.bfloat16)  21.1 us
  transfers between devices with their start and end apart: 4, of which 4 were waited for; matrix products, arithmetic and copies ran while one was open for 0% of the time, Pallas kernels for 0%

profile of v1, /device:TPU:0, one launch (start us, length us, event | category | flops | bytes accessed | tf_op | source)
XLA Modules:
  0.0 311.4 jit_solution(16682762255544478980)
XLA Ops:
  7.2 0.0 all-gather.2.cloned.1.call-start
  7.2 0.7 all-gather.2.cloned.1.call-update
  7.9 3.0 collective-permute-start
  10.9 2.5 collective-permute-done
  13.4 0.9 broadcast_select_fusion.5
  14.3 2.2 collective-permute-start.1
  16.4 2.9 collective-permute-done.1
  19.4 3.1 collective-permute-start.2
  22.5 9.6 %collective-permute-done.2 = bf16[4,128,256]{2,1,0:T(8,128)(2,1)S(1)} collective-permute-done((bf16[4,128,256]{2,1,0:T(8,128)(2,1)S(1)}, bf16[4,128,256]{2,1,0:T(8,128)(2,1)S(1)}, u32[]{:S(2)}, u32[]{:S(2)}) %collective-permute-start.2) | collective-permute-done | bytes 262176 | tf_op jit(solution)/shard_map/ppermute | solution.py:22
  32.2 0.2 multiply_reduce_fusion.1
  32.5 14.2 %all-gather.2.cloned.1.call-done = bf16[256,8192]{1,0:T(8,128)(2,1)} async-done(((bf16[64,8192]{1,0:T(8,128)(2,1)}), bf16[256,8192]{1,0:T(8,128)(2,1)}) %all-gather.2.cloned.1.call-update) | async-done | bytes 4194320 | tf_op jit(solution)/shard_map/all_gather | solution.py:42
  46.7 3.1 multiply_reduce_fusion
  49.8 17.7 %fusion.16 = (f32[8192]{0:T(1024)S(1)}, f32[1024,8192]{1,0:T(8,128)}) fusion(f32[8192]{0:T(1024)S(1)} %add_sqrt_fusion, f32[1024]{0:T(1024)S(1)} %sqrt_bitcast_fusion, bf16[1024,256]{1,0:T(8,128)(2,1)S(1)} %bitcast.8, bf16[256,8192]{1,0:T(8,128)(2,1)} %all-gather.2.cloned.1.call-done), kind=kOutput, calls=%fused_computation.37 | convolution fusion | flops 4328513536 | bytes 38342656 | tf_op jit(solution)/shard_map/dot_general | solution.py:44
  67.5 10.4 %psum.56 = f32[8192]{0:T(1024)S(1)} all-reduce(f32[8192]{0:T(1024)S(1)} %get-tuple-element.15), channel_id=1, replica_groups=mesh['batch'=4,'proto'=8] {'batch'}, use_global_device_ids=true, to_apply=%region_3.4 | all-reduce | flops 8192 | bytes 65536 | tf_op jit(solution)/shard_map/psum | solution.py:30
  77.9 12.2 %divide_reduce_fusion = f32[1024]{0:T(1024)S(1)} fusion(f32[1024,8192]{1,0:T(8,128)} %get-tuple-element.16, f32[8192]{0:T(1024)S(1)} %psum.56), kind=kLoop, calls=%fused_computation.16 | loop fusion | flops 16776192 | bytes 33591296 | tf_op jit(solution)/shard_map/reduce_sum | solution.py:35
  90.1 21.5 %psum.57 = f32[1024]{0:T(1024)S(1)} all-reduce(f32[1024]{0:T(1024)S(1)} %divide_reduce_fusion), channel_id=1, replica_groups=mesh['batch'=4,'proto'=8] {'proto'}, use_global_device_ids=true, to_apply=%region_5.6 | all-reduce | flops 1024 | bytes 8192 | tf_op jit(solution)/shard_map/psum | solution.py:35
  111.6 14.1 %fusion.11 = f32[8192]{0:T(1024)S(1)} fusion(f32[1024,8192]{1,0:T(8,128)} %get-tuple-element.16, f32[1024]{0:T(1024)S(1)} %psum.57, f32[8192]{0:T(1024)S(1)} %psum.56), kind=kLoop, calls=%fused_computation.17 | loop fusion | flops 25157632 | bytes 33624064 | tf_op jit(solution)/shard_map/reduce_sum | solution.py:30
  125.7 10.3 %psum.58 = f32[8192]{0:T(1024)S(1)} all-reduce(f32[8192]{0:T(1024)S(1)} %fusion.11), channel_id=1, replica_groups=mesh['batch'=4,'proto'=8] {'batch'}, use_global_device_ids=true, to_apply=%region_7.8 | all-reduce | flops 8192 | bytes 65536 | tf_op jit(solution)/shard_map/psum | solution.py:30
  136.0 14.1 %fusion.13 = f32[1024]{0:T(1024)S(1)} fusion(f32[1024,8192]{1,0:T(8,128)} %get-tuple-element.16, f32[8192]{0:T(1024)S(1)} %psum.58, f32[1024]{0:T(1024)S(1)} %psum.57, f32[8192]{0:T(1024)S(1)} %psum.56), kind=kLoop, calls=%fused_computation.19 | loop fusion | flops 33553408 | bytes 33628160 | tf_op jit(solution)/shard_map/reduce_sum | solution.py:35
  150.1 17.1 %psum.59 = f32[1024]{0:T(1024)S(1)} all-reduce(f32[1024]{0:T(1024)S(1)} %fusion.13), channel_id=1, replica_groups=mesh['batch'=4,'proto'=8] {'proto'}, use_global_device_ids=true, to_apply=%region_9.10 | all-reduce | flops 1024 | bytes 8192 | tf_op jit(solution)/shard_map/psum | solution.py:35
  167.3 14.5 %fusion.14 = f32[8192]{0:T(1024)S(1)} fusion(f32[1024,8192]{1,0:T(8,128)} %get-tuple-element.16, f32[1024]{0:T(1024)S(1)} %psum.59, f32[8192]{0:T(1024)S(1)} %psum.58, f32[1024]{0:T(1024)S(1)} %psum.57, f32[8192]{0:T(1024)S(1)} %psum.56), kind=kLoop, calls=%fused_computation.20 | loop fusion | flops 41934848 | bytes 33660928 | tf_op jit(solution)/shard_map/reduce_sum | solution.py:30
  181.7 10.4 %psum.60 = f32[8192]{0:T(1024)S(1)} all-reduce(f32[8192]{0:T(1024)S(1)} %fusion.14), channel_id=1, replica_groups=mesh['batch'=4,'proto'=8] {'batch'}, use_global_device_ids=true, to_apply=%region_11.12 | all-reduce | flops 8192 | bytes 65536 | tf_op jit(solution)/shard_map/psum | solution.py:30
  192.2 28.0 %broadcast_multiply_fusion = (f32[1024,8192]{1,0:T(8,128)}, f32[1024]{0:T(1024)S(1)}) fusion(f32[1024,8192]{1,0:T(8,128)} %get-tuple-element.16, f32[8192]{0:T(1024)S(1)} %psum.60, f32[1024]{0:T(1024)S(1)} %psum.59, f32[8192]{0:T(1024)S(1)} %psum.58, f32[1024]{0:T(1024)S(1)} %psum.57, f32[8192]{0:T(1024)S(1)} %psum.56), kind=kLoop, calls=%fused_computation.21 | loop fusion | flops 58719232 | bytes 67219456 | tf_op jit(solution)/shard_map/mul | solution.py:54
  220.2 27.8 %fusion.1 = (f32[2,1024]{1,0:T(2,128)S(1)}, f32[2,1024]{1,0:T(2,128)S(1)}) fusion(bf16[2,1024,8192]{2,1,0:T(8,128)(2,1)} %param.5, f32[1024,8192]{1,0:T(8,128)} %get-tuple-element.7), kind=kLoop, calls=%fused_computation.3 | loop fusion | flops 83881984 | bytes 67125248 | tf_op jit(solution)/shard_map/reduce_sum | solution.py:49
  248.0 34.9 %all-reduce = (f32[1024]{0:T(1024)S(1)}, f32[2,1024]{1,0:T(2,128)S(1)}, f32[2,1024]{1,0:T(2,128)S(1)}) all-reduce(f32[1024]{0:T(1024)S(1)} %get-tuple-element.8, f32[2,1024]{1,0:T(2,128)S(1)} %get-tuple-element.3, f32[2,1024]{1,0:T(2,128)S(1)} %get-tuple-element.2), channel_id=1, replica_groups=mesh['batch'=4,'proto'=8] {'proto'}, use_global_device_ids=true, to_apply=%region_13.14 | all-reduce | flops 5120 | bytes 40960 | tf_op jit(solution)/shard_map/psum | solution.py:55
  282.9 21.1 %fusion.12 = bf16[1024,8192]{1,0:T(8,128)(2,1)} fusion(f32[1024,8192]{1,0:T(8,128)} %get-tuple-element.16, f32[1024]{0:T(1024)S(1)} %get-tuple-element.4, f32[8192]{0:T(1024)S(1)} %psum.60, f32[1024]{0:T(1024)S(1)} %psum.59, f32[8192]{0:T(1024)S(1)} %psum.58, f32[1024]{0:T(1024)S(1)} %psum.57, f32[8192]{0:T(1024)S(1)} %psum.56), kind=kLoop, calls=%fused_computation.18 | loop fusion | flops 67108864 | bytes 50442240 | tf_op jit(solution)/shard_map/convert_element_type | solution.py:60
  303.9 0.6 divide_subtract_fusion
  (7 shorter events, 0.2 us)
Async XLA Ops:
  7.2 39.6 %all-gather.2.cloned.1.call-start = ((), (), s32[]{:S(2)}) async-start(), calls=%async_computation | async-start | bytes 5242880 | tf_op jit(solution)/shard_map/all_gather | solution.py:42
  7.9 5.5 %collective-permute-start = (bf16[1,128,256]{2,1,0:T(8,128)(2,1)}, bf16[1,128,256]{2,1,0:T(8,128)(2,1)S(1)}, u32[]{:S(2)}, u32[]{:S(2)}) collective-permute-start(bf16[1,128,256]{2,1,0:T(8,128)(2,1)} %bitcast.9), channel_id=1, source_target_pairs={{0,1},{1,0},{2,3},{3,2},{4,5},{5,4},{6,7},{7,6},{8,9},{9,8},{10,11... | collective-permute-start | bytes 196616 | tf_op jit(solution)/shard_map/ppermute | solution.py:22
  14.3 5.1 %collective-permute-start.1 = (bf16[2,128,256]{2,1,0:T(8,128)(2,1)S(1)}, bf16[2,128,256]{2,1,0:T(8,128)(2,1)S(1)}, u32[]{:S(2)}, u32[]{:S(2)}) collective-permute-start(bf16[2,128,256]{2,1,0:T(8,128)(2,1)S(1)} %pad_maximum_fusion.2), channel_id=1, source_target_pairs={{0,2},{1,3},{2,0},{3,1},{4,6},{5,7},{6,4},{7,5},{8,10},{9,11},{10,... | collective-permute-start | bytes 393224 | tf_op jit(solution)/shard_map/ppermute | solution.py:22
  19.4 12.7 %collective-permute-start.2 = (bf16[4,128,256]{2,1,0:T(8,128)(2,1)S(1)}, bf16[4,128,256]{2,1,0:T(8,128)(2,1)S(1)}, u32[]{:S(2)}, u32[]{:S(2)}) collective-permute-start(bf16[4,128,256]{2,1,0:T(8,128)(2,1)S(1)} %pad_maximum_fusion.1), channel_id=1, source_target_pairs={{0,4},{1,5},{2,6},{3,7},{4,0},{5,1},{6,2},{7,3},{8,12},{9,13},{10,... | collective-permute-start | bytes 786440 | tf_op jit(solution)/shard_map/ppermute | solution.py:22
Sparse Core Ops, SparseCore 0:
  9.5 37.1 all-gather.1
